TPU v7x, 256 devices: a whole 4x4x8 slice. The times are simulated.
256 devices in a mesh: dp: 4 (over x), context: 32 (over y, z), head: 2 (over core).
Axes of the slice: x: 4, y: 4, z: 8, core: 2. Of those that a mesh axis runs over, the one named last changes fastest.
Arguments:
- tokens: bfloat16 [4, 2, 4096, 4096], P('dp', None, 'context', 'head'), may hold values from -7 to 7
- queries: bfloat16 [4, 2, 4096, 2048], P('dp', None, 'context', 'head'), may hold values from -160 to 160
- grad_out: bfloat16 [4, 2, 4096, 2048], P('dp', None, 'context', 'head'), may hold values from -6 to 6
- w_key: bfloat16 [4096, 256], P('context', 'head'), may hold values from -0.09375 to 0.09375
- w_value: bfloat16 [4096, 256], P('context', 'head'), may hold values from -0.09375 to 0.09375
- block_len: int32 [4], P('dp'), may hold values from 8 to 32, as said below
Outputs:
- grad_query: bfloat16 [4, 2, 4096, 2048], P('dp', None, 'context', 'head')
- grad_x: bfloat16 [4, 2, 4096, 4096], P('dp', None, 'context', 'head')
- grad_wkey: float32 [4096, 256], P('context', 'head')
- grad_wvalue: float32 [4096, 256], P('context', 'head')
Inputs may be any that keep to these rules, and one draw needn't show every extreme that they name: `block_len`: each entry is 8, 16 or 32.
All inputs are finite; a program needn't handle non-finite values.
Results may differ from a plain program's by a relative error of at most 0.025.
Values may be sent and summed in bfloat16 or wider, within the bound.
No kernel may reach another device: no remote copies, remote signals or barrier semaphores. Data moves between devices by JAX's collectives and lax.ppermute only.
A program may use at most 64 MiB of HBM per device.

v0:
```python
import math
import jax
import jax.numpy as jnp
from jax import lax
from jax.sharding import Mesh
from jax.sharding import PartitionSpec as P

HEAD_DIM = 128
CONTEXT = ("context_0", "context_1")
masked_score = -1e30


def joined_along(tiles, dim):
    lengths = list(tiles.shape[1:])
    lengths[dim] *= tiles.shape[0]
    return jnp.moveaxis(tiles, 0, dim).reshape(lengths)


def sent_to_all(array, axis):
    copies = jnp.broadcast_to(array, (lax.axis_size(axis), *array.shape))
    return lax.all_to_all(copies, axis, split_axis=0, concat_axis=0, tiled=True)


def gather_directly(array, axis, dim):
    return joined_along(sent_to_all(array, axis), dim)


def summed_rows(array, axes, dim):
    for axis in axes:
        array = lax.psum_scatter(array, axis, scatter_dimension=dim, tiled=True)
    return array


def split_up(array, dim, peers):
    lengths = array.shape
    tiles = array.reshape(*lengths[:dim], peers, lengths[dim] // peers, *lengths[dim + 1 :])
    return jnp.moveaxis(tiles, dim, 0)


def summed_on_arrival(array, axis, dim):
    peers = lax.axis_size(axis)
    tiles = lax.all_to_all(split_up(array, dim, peers), axis, 0, 0, tiled=True)
    return jnp.sum(tiles.astype(jnp.float32), axis=0)


def sum_by_axis(terms, axes):
    so_far = terms.astype(jnp.bfloat16)
    for axis in axes:
        so_far = lax.psum_scatter(so_far, axis, scatter_dimension=0, tiled=True)
    return so_far.astype(jnp.float32)


def over_copies(array, axis):
    everything = sent_to_all(array, axis)
    return jnp.sum(everything.astype(jnp.float32), axis=0)


def score_block(query_rows, key_rows, score_scale):
    return (
        jnp.einsum("ikgd,jkd->kgij", query_rows, key_rows, preferred_element_type=jnp.float32)
        * score_scale
    )


def visible_mask(query_pos, key_pos, block_size, strict):
    query_block = query_pos // block_size
    key_block = key_pos // block_size
    if strict:
        return key_block[None, :] < query_block[:, None]
    return key_block[None, :] <= query_block[:, None]


def forward_step(carried, query_rows, key_rows, value_rows, allowed_mask, score_scale):
    row_peak, row_total, weighted = carried
    logits = jnp.where(allowed_mask, score_block(query_rows, key_rows, score_scale), masked_score)
    new_peak = jnp.maximum(row_peak, jnp.max(logits, axis=-1))
    shrink = jnp.exp(row_peak - new_peak)
    weights = jnp.where(allowed_mask, jnp.exp(logits - new_peak[..., None]), 0.0)
    row_total = row_total * shrink + jnp.sum(weights, axis=-1)
    update = jnp.einsum(
        "kgij,jkd->kgid",
        weights.astype(jnp.bfloat16),
        value_rows,
        preferred_element_type=jnp.float32,
    )
    return (new_peak, row_total, weighted * shrink[..., None] + update)


def backward_step(
    query_rows, grad_rows, key_rows, value_rows, allowed_mask, log_total, row_delta, score_scale
):
    logits = jnp.where(allowed_mask, score_block(query_rows, key_rows, score_scale), masked_score)
    probs = jnp.exp(logits - log_total[..., None])
    probs_half = probs.astype(jnp.bfloat16)
    grad_probs = jnp.einsum(
        "ikgd,jkd->kgij", grad_rows, value_rows, preferred_element_type=jnp.float32
    )
    grad_logits = (probs * (grad_probs - row_delta[..., None])).astype(jnp.bfloat16)
    grad_rows_query = jnp.einsum(
        "kgij,jkd->ikgd", grad_logits, key_rows, preferred_element_type=jnp.float32
    )
    grad_key = (
        jnp.einsum("kgij,ikgd->jkd", grad_logits, query_rows, preferred_element_type=jnp.float32)
        * score_scale
    )
    grad_value = jnp.einsum(
        "kgij,ikgd->jkd", probs_half, grad_rows, preferred_element_type=jnp.float32
    )
    return (grad_rows_query, grad_key, grad_value)


def finish_rows(carried, grad_rows):
    row_peak, row_total, weighted = carried
    outputs = weighted / row_total[..., None]
    row_delta = jnp.einsum("ikgd,kgid->kgi", grad_rows.astype(jnp.float32), outputs)
    return (row_peak + jnp.log(row_total), row_delta)


def per_device(tokens, queries, grad_out, w_key, w_value, block_len):
    cycle_size = lax.axis_size(CONTEXT)
    my_index = lax.axis_index(CONTEXT)
    shard_rows = tokens.shape[2]
    kv_width = w_key.shape[1]
    kv_local = kv_width // HEAD_DIM
    query_width = queries.shape[3]
    group_size = query_width // HEAD_DIM // kv_local
    score_scale = 1.0 / math.sqrt(HEAD_DIM)
    block_size = block_len[0]
    local_pos = lax.iota(jnp.int32, shard_rows)
    span_rows = min(cycle_size * shard_rows, max(512, shard_rows))
    full_tokens = gather_directly(tokens[0].reshape(2 * shard_rows, tokens.shape[3]), "head", 1)
    weight_pair = jnp.concatenate([w_key, w_value], axis=1)
    columns = full_tokens
    projected = jnp.dot(
        columns,
        lax.all_gather(weight_pair, CONTEXT, axis=0, tiled=True),
        preferred_element_type=jnp.float32,
    ).astype(jnp.bfloat16)
    clean_pairs = projected[:shard_rows]
    q_clean = queries[0, 0].reshape(shard_rows, kv_local, group_size, HEAD_DIM)
    g_clean = grad_out[0, 0].reshape(shard_rows, kv_local, group_size, HEAD_DIM)
    noisy_bundle = jnp.concatenate([queries[0, 1], grad_out[0, 1], projected[shard_rows:]], axis=1)
    q_noisy = noisy_bundle[:, :query_width].reshape(shard_rows, kv_local, group_size, HEAD_DIM)
    g_noisy = noisy_bundle[:, query_width : 2 * query_width].reshape(
        shard_rows, kv_local, group_size, HEAD_DIM
    )
    k_noisy = noisy_bundle[:, 2 * query_width : 2 * query_width + kv_width].reshape(
        shard_rows, kv_local, HEAD_DIM
    )
    v_noisy = noisy_bundle[:, 2 * query_width + kv_width :].reshape(shard_rows, kv_local, HEAD_DIM)
    clean_pos = my_index * shard_rows + local_pos
    noisy_pos = my_index * shard_rows + local_pos
    own_block = local_pos // block_size
    same_block = own_block[None, :] == own_block[:, None]
    clean_limit = (my_index + 1) * shard_rows
    noisy_limit = (my_index + 1) * shard_rows
    state_shape = (kv_local, group_size, shard_rows)
    empty_state = (
        jnp.full(state_shape, masked_score, jnp.float32),
        jnp.zeros(state_shape, jnp.float32),
        jnp.zeros(state_shape + (HEAD_DIM,), jnp.float32),
    )
    noisy_start = forward_step(empty_state, q_noisy, k_noisy, v_noisy, same_block, score_scale)
    block_turns = (jnp.maximum(clean_limit, noisy_limit) + span_rows - 1) // span_rows

    def split_pairs(pair_rows):
        count_rows = pair_rows.shape[0]
        key_rows = pair_rows[:, :kv_width].reshape(count_rows, kv_local, HEAD_DIM)
        value_rows = pair_rows[:, kv_width:].reshape(count_rows, kv_local, HEAD_DIM)
        return (key_rows, value_rows)

    carried = (empty_state, noisy_start)
    pair_rows = gather_directly(clean_pairs, CONTEXT, 0)
    first_row = jnp.int32(0)
    key_rows, value_rows = split_pairs(pair_rows)
    key_pos = lax.iota(jnp.int32, pair_rows.shape[0])
    clean_mask = visible_mask(clean_pos, key_pos, block_size, False)
    noisy_mask = visible_mask(noisy_pos, key_pos, block_size, True)

    def clean_update():
        return forward_step(carried[0], q_clean, key_rows, value_rows, clean_mask, score_scale)

    def clean_keep():
        return carried[0]

    def noisy_update():
        return forward_step(carried[1], q_noisy, key_rows, value_rows, noisy_mask, score_scale)

    def noisy_keep():
        return carried[1]

    clean_state = lax.cond(first_row < clean_limit, clean_update, clean_keep)
    noisy_state = lax.cond(first_row < noisy_limit, noisy_update, noisy_keep)
    clean_lse, clean_delta = finish_rows(clean_state, g_clean)
    noisy_lse, noisy_delta = finish_rows(noisy_state, g_noisy)
    pairs_back = lax.all_gather(clean_pairs, CONTEXT, axis=0, tiled=True)
    query_zero = jnp.zeros((shard_rows, kv_local, group_size, HEAD_DIM), jnp.float32)

    def backward_turn(turn_index, carried):
        query_grads, pair_total = carried
        first_row = turn_index * span_rows
        pair_rows = lax.dynamic_slice_in_dim(pairs_back, first_row, span_rows, 0)
        key_rows, value_rows = split_pairs(pair_rows)
        key_pos = first_row + lax.iota(jnp.int32, span_rows)
        clean_mask = visible_mask(clean_pos, key_pos, block_size, False)
        noisy_mask = visible_mask(noisy_pos, key_pos, block_size, True)
        pair_zero = jnp.zeros((span_rows, kv_local, HEAD_DIM), jnp.float32)

        def clean_work():
            return backward_step(
                q_clean,
                g_clean,
                key_rows,
                value_rows,
                clean_mask,
                clean_lse,
                clean_delta,
                score_scale,
            )

        def noisy_work():
            return backward_step(
                q_noisy,
                g_noisy,
                key_rows,
                value_rows,
                noisy_mask,
                noisy_lse,
                noisy_delta,
                score_scale,
            )

        def no_work():
            return (query_zero, pair_zero, pair_zero)

        clean_dq, clean_dk, clean_dv = lax.cond(first_row < clean_limit, clean_work, no_work)
        noisy_dq, noisy_dk, noisy_dv = lax.cond(first_row < noisy_limit, noisy_work, no_work)
        pair_grads = jnp.concatenate(
            [
                (clean_dk + noisy_dk).reshape(span_rows, kv_width),
                (clean_dv + noisy_dv).reshape(span_rows, kv_width),
            ],
            axis=1,
        )
        previous = lax.dynamic_slice_in_dim(pair_total, first_row, span_rows, 0)
        pair_total = lax.dynamic_update_slice_in_dim(
            pair_total, previous + pair_grads, first_row, 0
        )
        return ((query_grads[0] + clean_dq, query_grads[1] + noisy_dq), pair_total)

    pair_empty = jnp.zeros((cycle_size * shard_rows, 2 * kv_width), jnp.float32)
    query_grads, pair_total = lax.fori_loop(
        0, block_turns, backward_turn, ((query_zero, query_zero), pair_empty)
    )
    clean_pair_grads = (
        summed_rows(pair_total.astype(jnp.bfloat16), CONTEXT, 0)
        .astype(jnp.float32)
        .astype(jnp.bfloat16)
    )
    own_dq, own_dk, own_dv = backward_step(
        q_noisy, g_noisy, k_noisy, v_noisy, same_block, noisy_lse, noisy_delta, score_scale
    )
    dq_clean = (query_grads[0] * score_scale).astype(jnp.bfloat16).reshape(shard_rows, query_width)
    dq_noisy = (
        ((query_grads[1] + own_dq) * score_scale)
        .astype(jnp.bfloat16)
        .reshape(shard_rows, query_width)
    )
    noisy_pair = jnp.concatenate(
        [own_dk.reshape(shard_rows, kv_width), own_dv.reshape(shard_rows, kv_width)], axis=1
    ).astype(jnp.bfloat16)
    return_bundle = jnp.concatenate([dq_noisy, noisy_pair], axis=1)
    dq_noisy = return_bundle[:, :query_width]
    noisy_pair = return_bundle[:, query_width:]
    pair_grads = jnp.concatenate([clean_pair_grads, noisy_pair], axis=0)
    input_terms = jnp.einsum(
        "tc,rc->tr",
        pair_grads,
        lax.all_gather(weight_pair, CONTEXT, axis=0, tiled=True),
        preferred_element_type=jnp.float32,
    )
    grad_x = (
        summed_on_arrival(input_terms.astype(jnp.bfloat16), "head", 1)
        .astype(jnp.bfloat16)
        .reshape(tokens.shape)
    )
    columns = full_tokens
    weight_local = sum_by_axis(
        jnp.einsum("tr,tc->rc", columns, pair_grads, preferred_element_type=jnp.float32), CONTEXT
    )
    weight_sums = over_copies(weight_local.astype(jnp.bfloat16), "dp").astype(jnp.float32)
    grad_query = jnp.stack([dq_clean, dq_noisy])[None]
    return (grad_query, grad_x, weight_sums[:, :kv_width], weight_sums[:, kv_width:])


def solution(mesh):
    torus = Mesh(
        mesh.devices.reshape(mesh.shape["dp"], 4, 8, mesh.shape["head"]),
        ("dp", "context_0", "context_1", "head"),
    )
    in_specs = (
        P("dp", None, CONTEXT, "head"),
        P("dp", None, CONTEXT, "head"),
        P("dp", None, CONTEXT, "head"),
        P(CONTEXT, "head"),
        P(CONTEXT, "head"),
        P("dp"),
    )
    out_specs = (
        P("dp", None, CONTEXT, "head"),
        P("dp", None, CONTEXT, "head"),
        P(CONTEXT, "head"),
        P(CONTEXT, "head"),
    )
    return jax.shard_map(
        per_device, mesh=torus, in_specs=in_specs, out_specs=out_specs, check_vma=False
    )
```

profile of v0, /device:TPU:8, one launch (start us, length us, event | category | flops | bytes accessed | tf_op | source)
XLA Modules:
  0.0 507.5 jit_solution(627499071341025403)
XLA Ops:
  10.3 5.4 %all_to_all.20 = bf16[2,256,2048]{1,2,0:T(8,128)(2,1)S(1)} all-to-all(bf16[2,256,2048]{1,2,0:T(8,128)(2,1)S(1)} %broadcast_in_dim.134), channel_id=1, replica_groups=mesh['dp'=4,'context_0'=4,'context_1'=8,'head'=2] {'head'}, dimensions={0} | all-to-all | bytes 4194304 | tf_op jit(solution)/shard_map/all_to_all | solution.py:21
  15.7 75.1 %all-gather.3.cloned.1.call-done = bf16[4096,256]{1,0:T(8,128)(2,1)} async-done(((bf16[128,256]{1,0:T(8,128)(2,1)}), bf16[4096,256]{1,0:T(8,128)(2,1)}) %all-gather.3.cloned.1.call-update) | async-done | bytes 2097168 | tf_op jit(solution)/shard_map/all_gather | solution.py:136
  94.9 7.3 %all-to-all-start.1 = ((bf16[32,128,256]{2,1,0:T(8,128)(2,1)}), bf16[32,128,256]{2,1,0:T(8,128)(2,1)}, u32[]{:S(2)}, u32[]{:S(2)}) async-start(bf16[32,128,256]{2,1,0:T(8,128)(2,1)} %broadcast_in_dim.135), calls=%async_computation.1 | async-start | bytes 4194304 | tf_op jit(solution)/shard_map/all_to_all | solution.py:21
  112.4 35.9 %all-to-all-done.1 = bf16[32,128,256]{2,1,0:T(8,128)(2,1)} async-done(((bf16[32,128,256]{2,1,0:T(8,128)(2,1)}), bf16[32,128,256]{2,1,0:T(8,128)(2,1)}, u32[]{:S(2)}, u32[]{:S(2)}) %all-to-all-start.1) | async-done | bytes 2097184 | tf_op jit(solution)/shard_map/all_to_all | solution.py:21
  151.6 18.4 %conditional.5 = (f32[1,8,128]{2,1,0:T(8,128)}, f32[1,8,128]{2,1,0:T(8,128)S(1)}, f32[1,8,128,128]{3,2,1,0:T(8,128)S(1)}, f32[1,8,128]{2,1,0:T(8,128)}) conditional(s32[]{:T(128)} %convert_element_type.79, (f32[1,8,128]{2,1,0:T(8,128)}, f32[1,8,128]{2,1,0:T(8,128)S(1)}, f32[1,8,128,128]{3,2,1,0:T(8,128)S(1)}) %tuple.160, (s32[4096]{0:T(1024)S(1)}, ...), branch_computations={%region_6.7_spmd, %region_7.10_spmd} | conditional | flops 2202799104 | bytes 58019872 | solution.py:193
  158.0 4.0 fusion.27
  163.3 6.0 %fusion.35 = f32[1,8,128,128]{3,2,1,0:T(8,128)S(1)} fusion(f32[4096,128,8]{1,0,2:T(8,128)S(1)} %get-tuple-element.709, f32[8,128]{1,0:T(8,128)S(1)} %bitcast.427, pred[128,4096]{0,1:T(8,128)(4,1)S(1)} %broadcast_compare_fusion.1, bf16[4096,1,128]{2,0,1:T(8,128)(2,1)} %get-tuple-element.377, f32[1,8,128,128]{3,2,1,0:T(8,128)S(1)} %get-tuple-element.376, ...), kind=kOutput, calls=%fused_computation.33 | convolution fusion | flops 1094975488 | bytes 19406848 | tf_op jit(solution)/shard_map/cond/branch_1_fun/kgij,jkd->kgid/dot_general | solution.py:80
  173.0 15.9 %conditional.4 = (f32[1,8,128]{2,1,0:T(8,128)S(1)}, f32[1,8,128]{2,1,0:T(8,128)S(1)}, f32[1,8,128,128]{3,2,1,0:T(8,128)S(1)}, f32[1,8,128]{2,1,0:T(8,128)S(1)}) conditional(s32[]{:T(128)} %convert_element_type.79, () %tuple.57, (s32[4096]{0:T(1024)S(1)}, s32[128,4096]{0,1:T(8,128)S(1)}, bf16[4096,1,128]{2,0,1:T(8,128)(2,1)}, ...), branch_computations={%region_0.1_spmd, %region_1.4_spmd} | conditional | flops 2202670080 | bytes 57479200 | solution.py:192
  178.6 4.2 fusion.6
  182.9 6.0 %fusion.14 = f32[1,8,128,128]{3,2,1,0:T(8,128)S(1)} fusion(f32[4096,128,8]{1,0,2:T(8,128)S(1)} %get-tuple-element.707, f32[8,128]{1,0:T(8,128)S(1)} %get-tuple-element.705, pred[128,4096]{0,1:T(8,128)(4,1)S(1)} %broadcast_compare_fusion, bf16[4096,1,128]{2,0,1:T(8,128)(2,1)} %get-tuple-element.369, f32[8,128]{1,0:T(8,128)S(1)} %get-tuple-element.704), kind=kOutput, calls=%fused_computation.11 | convolution fusion | flops 1094844416 | bytes 18882560 | tf_op jit(solution)/shard_map/cond/branch_1_fun/kgij,jkd->kgid/dot_general | solution.py:80
  195.3 54.1 %while.20 = (s32[]{:T(128)}, f32[128,1,8,128]{3,0,2,1:T(8,128)}, f32[128,1,8,128]{3,0,2,1:T(8,128)}, f32[4096,256]{0,1:T(8,128)}, s32[]{:T(128)}, /*index=5*/s32...) while((s32[]{:T(128)}, f32[128,1,8,128]{3,0,2,1:T(8,128)}, ...), condition=%wide.region_15.16_spmd.clone.clone, body=%wide.region_10.15_spmd.clone.clone.sunk | while | flops 1350440704 | bytes 36462060 | solution.py:252
  198.1 4.5 conditional.13
  202.6 4.5 conditional.12
  216.2 4.5 conditional.13
  220.6 4.5 conditional.12
  234.2 4.5 conditional.13
  238.7 4.5 conditional.12
  249.4 4.0 convert_element_type.84
  253.4 119.5 %reduce-scatter.9.cloned.1.call-done = bf16[1024,256]{0,1:T(8,128)(2,1)} async-done(((bf16[4096,256]{0,1:T(8,128)(2,1)}), bf16[1024,256]{0,1:T(8,128)(2,1)}) %reduce-scatter.9.cloned.1.call-update) | async-done | bytes 524304 | tf_op jit(solution)/shard_map/reduce_scatter | solution.py:30
  376.1 37.6 %reduce-scatter.13.cloned.1.call-done = bf16[128,256]{1,0:T(8,128)(2,1)} async-done(((bf16[1024,256]{1,0:T(8,128)(2,1)}), bf16[128,256]{1,0:T(8,128)(2,1)}) %reduce-scatter.13.cloned.1.call-update) | async-done | bytes 65552
  416.9 29.8 %reduce-scatter.11.cloned.1.call-done = bf16[1024,256]{0,1:T(8,128)(2,1)} async-done(((bf16[4096,256]{0,1:T(8,128)(2,1)}), bf16[1024,256]{0,1:T(8,128)(2,1)}) %reduce-scatter.11.cloned.1.call-update) | async-done | bytes 524304 | tf_op jit(solution)/shard_map/reduce_scatter | solution.py:49
  453.0 5.4 %all_to_all.21 = bf16[2,256,2048]{2,1,0:T(8,128)(2,1)S(1)} all-to-all(bf16[2,256,2048]{2,1,0:T(8,128)(2,1)S(1)} %bitcast.403), channel_id=1, replica_groups=mesh['dp'=4,'context_0'=4,'context_1'=8,'head'=2] {'head'}, dimensions={0} | all-to-all | bytes 4194304 | tf_op jit(solution)/shard_map/all_to_all | solution.py:42
  458.4 29.1 %reduce-scatter.15.cloned.1.call-done = bf16[128,256]{1,0:T(8,128)(2,1)} async-done(((bf16[1024,256]{1,0:T(8,128)(2,1)}), bf16[128,256]{1,0:T(8,128)(2,1)}) %reduce-scatter.15.cloned.1.call-update) | async-done | bytes 65552 | tf_op jit(solution)/shard_map/reduce_scatter | solution.py:49
  489.1 4.2 all-to-all-start.3
  (200 shorter events, 118.2 us)
Async XLA Ops:
  7.2 83.7 %all-gather.3.cloned.1.call-start = ((), (), s32[]{:S(2)}) async-start(), calls=%async_computation.8 | async-start | bytes 2162688 | tf_op jit(solution)/shard_map/all_gather | solution.py:136
  15.7 79.2 %copy-start.4 = (bf16[2,256,2048]{1,2,0:T(8,128)(2,1)}, bf16[2,256,2048]{1,2,0:T(8,128)(2,1)S(1)}, u32[]{:S(2)}) copy-start(bf16[2,256,2048]{1,2,0:T(8,128)(2,1)S(1)} %all_to_all.20) | copy-start | bytes 6291460
  93.2 11.9 %copy-start.16 = (bf16[256,256]{0,1:T(8,128)(2,1)}, bf16[256,256]{0,1:T(8,128)(2,1)S(1)}, u32[]{:S(2)}) copy-start(bf16[256,256]{0,1:T(8,128)(2,1)S(1)} %fusion.92) | copy-start | bytes 393220
  93.2 10.5 %copy-start.15 = (bf16[1,2,128,1024]{3,2,1,0:T(8,128)(2,1)S(1)}, bf16[1,2,128,1024]{3,2,1,0:T(8,128)(2,1)}, u32[]{:S(2)}) copy-start(bf16[1,2,128,1024]{3,2,1,0:T(8,128)(2,1)} %param.17) | copy-start | bytes 1572868
  93.2 9.0 %copy-start.14 = (bf16[128,256]{0,1:T(8,128)(2,1)}, bf16[128,256]{0,1:T(8,128)(2,1)S(1)}, u32[]{:S(2)}) copy-start(bf16[128,256]{0,1:T(8,128)(2,1)S(1)} %slice.67) | copy-start | bytes 196612
  94.9 53.4 %all-to-all-start.1 = ((bf16[32,128,256]{2,1,0:T(8,128)(2,1)}), bf16[32,128,256]{2,1,0:T(8,128)(2,1)}, u32[]{:S(2)}, u32[]{:S(2)}) async-start(bf16[32,128,256]{2,1,0:T(8,128)(2,1)} %broadcast_in_dim.135), calls=%async_computation.1 | async-start | bytes 4194304 | tf_op jit(solution)/shard_map/all_to_all | solution.py:21
  102.2 89.0 %all-gather.5.cloned.1.call-start = ((), (), s32[]{:S(2)}) async-start(), calls=%async_computation.9 | async-start | bytes 2162688 | tf_op jit(solution)/shard_map/all_gather | solution.py:196
  103.0 269.9 %reduce-scatter.9.cloned.1.call-start = ((), (), s32[]{:S(2)}) async-start(), calls=%async_computation.10 | async-start | bytes 2621440 | tf_op jit(solution)/shard_map/reduce_scatter | solution.py:30
  103.9 47.7 %copy-start.8 = (bf16[1,1,128,1024]{2,3,1,0:T(8,128)(2,1)}, bf16[1,1,128,1024]{2,3,1,0:T(8,128)(2,1)S(1)}, u32[]{:S(2)}) copy-start(bf16[1,1,128,1024]{2,3,1,0:T(8,128)(2,1)S(1)} %copy.165) | copy-start | bytes 786436
  105.1 5.6 %copy-start.17 = (bf16[256,256]{0,1:T(8,128)(2,1)S(1)}, bf16[256,256]{0,1:T(8,128)(2,1)}, u32[]{:S(2)}) copy-start(bf16[256,256]{0,1:T(8,128)(2,1)} %copy-done.16) | copy-start | bytes 393220
  105.3 84.7 %copy-start.6 = (bf16[1,1,128,1024]{2,3,1,0:T(8,128)(2,1)}, bf16[1,1,128,1024]{2,3,1,0:T(8,128)(2,1)S(1)}, u32[]{:S(2)}) copy-start(bf16[1,1,128,1024]{2,3,1,0:T(8,128)(2,1)S(1)} %copy.166) | copy-start | bytes 786436
  148.3 3.2 copy-start.18
  249.4 126.0 %copy-start.3 = (f32[1,8,128,128]{2,3,1,0:T(8,128)S(1)}, f32[1,8,128,128]{2,3,1,0:T(8,128)}, u32[]{:S(2)}) copy-start(f32[1,8,128,128]{2,3,1,0:T(8,128)} %copy-done.2) | copy-start | bytes 1572868
  249.4 126.0 %copy-start.7 = (bf16[1,1,128,1024]{2,3,1,0:T(8,128)(2,1)S(1)}, bf16[1,1,128,1024]{2,3,1,0:T(8,128)(2,1)}, u32[]{:S(2)}) copy-start(bf16[1,1,128,1024]{2,3,1,0:T(8,128)(2,1)} %copy-done.6) | copy-start | bytes 786436
  249.4 126.2 %copy-start.9 = (bf16[1,1,128,1024]{2,3,1,0:T(8,128)(2,1)S(1)}, bf16[1,1,128,1024]{2,3,1,0:T(8,128)(2,1)}, u32[]{:S(2)}) copy-start(bf16[1,1,128,1024]{2,3,1,0:T(8,128)(2,1)} %copy-done.8) | copy-start | bytes 786436
  253.4 161.3 %copy-start.5 = (bf16[2,256,2048]{1,2,0:T(8,128)(2,1)S(1)}, bf16[2,256,2048]{1,2,0:T(8,128)(2,1)}, u32[]{:S(2)}) copy-start(bf16[2,256,2048]{1,2,0:T(8,128)(2,1)} %copy-done.4) | copy-start | bytes 6291460
  253.4 160.4 %reduce-scatter.13.cloned.1.call-start = ((), (), s32[]{:S(2)}) async-start(), calls=%async_computation.12 | async-start | bytes 589824
  375.0 71.7 %reduce-scatter.11.cloned.1.call-start = ((), (), s32[]{:S(2)}) async-start(), calls=%async_computation.11 | async-start | bytes 2621440 | tf_op jit(solution)/shard_map/reduce_scatter | solution.py:49
  376.1 72.7 %copy-start.1 = (f32[128,1,8,128]{3,0,2,1:T(8,128)S(1)}, f32[128,1,8,128]{3,0,2,1:T(8,128)}, u32[]{:S(2)}) copy-start(f32[128,1,8,128]{3,0,2,1:T(8,128)} %get-tuple-element.441) | copy-start | bytes 1572868
  414.7 35.1 %copy-start = (f32[128,1,8,128]{3,0,2,1:T(8,128)S(1)}, f32[128,1,8,128]{3,0,2,1:T(8,128)}, u32[]{:S(2)}) copy-start(f32[128,1,8,128]{3,0,2,1:T(8,128)} %get-tuple-element.440) | copy-start | bytes 1572868
  416.8 35.2 %copy-start.11 = (bf16[4096,256]{1,0:T(8,128)(2,1)S(1)}, bf16[4096,256]{1,0:T(8,128)(2,1)}, u32[]{:S(2)}) copy-start(bf16[4096,256]{1,0:T(8,128)(2,1)} %all-gather.3.cloned.1.call-done) | copy-start | bytes 6291460
  416.8 70.7 %reduce-scatter.15.cloned.1.call-start = ((), (), s32[]{:S(2)}) async-start(), calls=%async_computation.13 | async-start | bytes 589824 | tf_op jit(solution)/shard_map/reduce_scatter | solution.py:49
  452.7 40.6 %copy-start.13 = (bf16[128,1,8,128]{0,3,2,1:T(8,128)(2,1)S(1)}, bf16[128,1,8,128]{0,3,2,1:T(8,128)(2,1)}, u32[]{:S(2)}) copy-start(bf16[128,1,8,128]{0,3,2,1:T(8,128)(2,1)} %fusion.88) | copy-start | bytes 786436
  489.1 10.9 %all-to-all-start.3 = ((bf16[4,128,256]{2,1,0:T(8,128)(2,1)}), bf16[4,128,256]{2,1,0:T(8,128)(2,1)S(1)}, u32[]{:S(2)}, u32[]{:S(2)}) async-start(bf16[4,128,256]{2,1,0:T(8,128)(2,1)} %broadcast_in_dim.144), calls=%async_computation.5 | async-start | bytes 524288 | tf_op jit(solution)/shard_map/all_to_all | solution.py:21
  (4 other events, 9.2 us)
Sparse Core Ops, SparseCore 0:
  11.2 79.6 all-gather.2
  106.1 83.5 all-gather.4
  253.5 119.3 reduce-scatter.8
  375.4 38.2 reduce-scatter.12
  417.0 29.7 reduce-scatter.10
  449.2 38.2 reduce-scatter.14
where the time goes:
time: 511 us; the launch traced here: 508 us
  waiting for transfers between devices  332 us (65%)
  matrix products  55.1 us (11%)
  other arithmetic  44.8 us (9%)
  local copies, waits for them, and re-layouts  37.4 us (7%)
  between operations  15.2 us (3%)
  starting transfers between devices  12 us (2%)
  blocking collectives  10.8 us (2%)
    reduce_scatter x1, waiting for transfers between devices, summed_rows(): array = lax.psum_scatter(array, axis, scatter_dimension=dim, tiled=True)  119 us
    all_gather x1, waiting for transfers between devices, per_device(): lax.all_gather(weight_pair, CONTEXT, axis=0, tiled=True)  75.1 us
    reduce_scatter x2, waiting for transfers between devices, sum_by_axis(): so_far = lax.psum_scatter(so_far, axis, scatter_dimension=0, tiled=True)  58.9 us
    all_to_all x2, waiting for transfers between devices, sent_to_all(): return lax.all_to_all(copies, axis, split_axis=0, concat_axis=0, tiled=True)  39.7 us
    unnamed x7, waiting for transfers between devices  38.4 us
    dot_general x9, matrix products, score_block(): jnp.einsum('ikgd,jkd->kgij', query_rows, key_rows, preferred_element_type...  17.7 us
    dot_general x3, matrix products, forward_step(): jnp.einsum('kgij,jkd->kgid', weights.astype(jnp.bfloat16), value_rows, pr...  13.1 us
    all_to_all x2, starting transfers between devices, sent_to_all(): return lax.all_to_all(copies, axis, split_axis=0, concat_axis=0, tiled=True)  11.5 us
  transfers between devices with their start and end apart: 8, of which 7 were waited for; matrix products, arithmetic and copies ran while one was open for 12% of the time, Pallas kernels for 0%

commit v1 on v0

--- a/solution.py
+++ b/solution.py
@@ -133,7 +133,9 @@
     columns = full_tokens
     projected = jnp.dot(
         columns,
-        lax.all_gather(weight_pair, CONTEXT, axis=0, tiled=True),
+        jnp.concatenate(
+            lax.all_to_all(jnp.stack([weight_pair] * lax.axis_size(CONTEXT)), CONTEXT, 0, 0), axis=0
+        ),
         preferred_element_type=jnp.float32,
     ).astype(jnp.bfloat16)
     clean_pairs = projected[:shard_rows]

time: 511 us -> 577 us (1.13)
  blocking collectives: 10.8 us -> 65.8 us
  waiting for transfers between devices: 332 us -> 340 us
    all_to_all x1, blocking collectives: 5.42 us -> 60.4 us  [per_device(): lax.all_to_all(jnp.stack([weight_pair] * lax.axis_size(CONTEXT)), CONTEXT...]
    all_to_all x2 -> x3, waiting for transfers between devices: 39.7 us -> 44.4 us  [sent_to_all(): return lax.all_to_all(copies, axis, split_axis=0, concat_axis=0, tiled=True)]
    all_to_all x2 -> x3, starting transfers between devices: 11.5 us -> 15.6 us  [sent_to_all(): return lax.all_to_all(copies, axis, split_axis=0, concat_axis=0, tiled=True)]
  transfers between devices with their start and end apart: 8 -> 9, of which waited for: 7 -> 8; matrix products, arithmetic and copies ran while one was open for 12% -> 11% of each run, Pallas kernels for 0% -> 0%
where the time goes in v1:
time: 577 us; the launch traced here: 574 us
  waiting for transfers between devices  340 us (59%)
  blocking collectives  65.8 us (11%)
  matrix products  54.7 us (9%)
  other arithmetic  43.3 us (8%)
  local copies, waits for them, and re-layouts  38.4 us (7%)
  starting transfers between devices  16.1 us (3%)
  between operations  15.3 us (3%)
    reduce_scatter x1, waiting for transfers between devices, summed_rows(): array = lax.psum_scatter(array, axis, scatter_dimension=dim, tiled=True)  120 us
    all_gather x1, waiting for transfers between devices, per_device(): lax.all_gather(weight_pair, CONTEXT, axis=0, tiled=True)  76.9 us
    all_to_all x1, blocking collectives, per_device(): lax.all_to_all(jnp.stack([weight_pair] * lax.axis_size(CONTEXT)), CONTEXT...  60.4 us
    reduce_scatter x2, waiting for transfers between devices, sum_by_axis(): so_far = lax.psum_scatter(so_far, axis, scatter_dimension=0, tiled=True)  59.3 us
    all_to_all x3, waiting for transfers between devices, sent_to_all(): return lax.all_to_all(copies, axis, split_axis=0, concat_axis=0, tiled=True)  44.4 us
    unnamed x7, waiting for transfers between devices  39 us
    dot_general x9, matrix products, score_block(): jnp.einsum('ikgd,jkd->kgij', query_rows, key_rows, preferred_element_type...  17.7 us
    all_to_all x3, starting transfers between devices, sent_to_all(): return lax.all_to_all(copies, axis, split_axis=0, concat_axis=0, tiled=True)  15.6 us
  transfers between devices with their start and end apart: 9, of which 8 were waited for; matrix products, arithmetic and copies ran while one was open for 11% of the time, Pallas kernels for 0%

profile of v1, /device:TPU:8, one launch (start us, length us, event | category | flops | bytes accessed | tf_op | source)
XLA Modules:
  0.0 573.8 jit_solution(4197930967370982670)
XLA Ops:
  17.0 60.4 %all_to_all.25 = bf16[32,128,256]{2,1,0:T(8,128)(2,1)S(1)} all-to-all(bf16[32,128,256]{2,1,0:T(8,128)(2,1)S(1)} %stack.4), channel_id=1, replica_groups=mesh['dp'=4,'context_0'=4,'context_1'=8,'head'=2] {'context_0','context_1'}, dimensions={0} | all-to-all | bytes 4194304 | tf_op jit(solution)/shard_map/all_to_all | solution.py:137
  79.9 7.6 %all-to-all-start.2 = ((bf16[32,128,256]{2,1,0:T(8,128)(2,1)}), bf16[32,128,256]{2,1,0:T(8,128)(2,1)S(1)}, u32[]{:S(2)}, u32[]{:S(2)}) async-start(bf16[32,128,256]{2,1,0:T(8,128)(2,1)} %broadcast_in_dim.135), calls=%async_computation.2 | async-start | bytes 4194304 | tf_op jit(solution)/shard_map/all_to_all | solution.py:21
  99.5 37.9 %all-to-all-done.2 = bf16[32,128,256]{2,1,0:T(8,128)(2,1)S(1)} async-done(((bf16[32,128,256]{2,1,0:T(8,128)(2,1)}), bf16[32,128,256]{2,1,0:T(8,128)(2,1)S(1)}, u32[]{:S(2)}, u32[]{:S(2)}) %all-to-all-start.2) | async-done | bytes 2097184 | tf_op jit(solution)/shard_map/all_to_all | solution.py:21
  139.0 18.3 %conditional.5 = (f32[1,8,128]{2,1,0:T(8,128)}, f32[1,8,128]{2,1,0:T(8,128)S(1)}, f32[1,8,128,128]{3,2,1,0:T(8,128)S(1)}, f32[1,8,128]{2,1,0:T(8,128)}) conditional(s32[]{:T(128)} %convert_element_type.79, (f32[1,8,128]{2,1,0:T(8,128)}, f32[1,8,128]{2,1,0:T(8,128)S(1)}, f32[1,8,128,128]{3,2,1,0:T(8,128)S(1)}) %tuple.160, (s32[4096]{0:T(1024)S(1)}, ...), branch_computations={%region_6.7_spmd, %region_7.10_spmd} | conditional | flops 2202799104 | bytes 58019872 | solution.py:195
  145.5 4.0 fusion.27
  150.8 6.0 %fusion.35 = f32[1,8,128,128]{3,2,1,0:T(8,128)S(1)} fusion(f32[4096,128,8]{1,0,2:T(8,128)S(1)} %get-tuple-element.709, f32[8,128]{1,0:T(8,128)S(1)} %bitcast.430, pred[128,4096]{0,1:T(8,128)(4,1)S(1)} %broadcast_compare_fusion.1, bf16[4096,1,128]{2,0,1:T(8,128)(2,1)} %get-tuple-element.377, f32[1,8,128,128]{3,2,1,0:T(8,128)S(1)} %get-tuple-element.376, ...), kind=kOutput, calls=%fused_computation.33 | convolution fusion | flops 1094975488 | bytes 19406848 | tf_op jit(solution)/shard_map/cond/branch_1_fun/kgij,jkd->kgid/dot_general | solution.py:80
  160.4 15.8 %conditional.4 = (f32[1,8,128]{2,1,0:T(8,128)S(1)}, f32[1,8,128]{2,1,0:T(8,128)S(1)}, f32[1,8,128,128]{3,2,1,0:T(8,128)S(1)}, f32[1,8,128]{2,1,0:T(8,128)S(1)}) conditional(s32[]{:T(128)} %convert_element_type.79, () %tuple.57, (s32[4096]{0:T(1024)S(1)}, s32[128,4096]{0,1:T(8,128)S(1)}, bf16[4096,1,128]{2,0,1:T(8,128)(2,1)}, ...), branch_computations={%region_0.1_spmd, %region_1.4_spmd} | conditional | flops 2202670080 | bytes 57479200 | solution.py:194
  166.0 4.2 fusion.6
  170.3 5.9 %fusion.14 = f32[1,8,128,128]{3,2,1,0:T(8,128)S(1)} fusion(f32[4096,128,8]{1,0,2:T(8,128)S(1)} %get-tuple-element.707, f32[8,128]{1,0:T(8,128)S(1)} %get-tuple-element.705, pred[128,4096]{0,1:T(8,128)(4,1)S(1)} %broadcast_compare_fusion, bf16[4096,1,128]{2,0,1:T(8,128)(2,1)} %get-tuple-element.369, f32[8,128]{1,0:T(8,128)S(1)} %get-tuple-element.704), kind=kOutput, calls=%fused_computation.11 | convolution fusion | flops 1094844416 | bytes 18882560 | tf_op jit(solution)/shard_map/cond/branch_1_fun/kgij,jkd->kgid/dot_general | solution.py:80
  182.6 54.1 %while.20 = (s32[]{:T(128)}, f32[128,1,8,128]{3,0,2,1:T(8,128)}, f32[128,1,8,128]{3,0,2,1:T(8,128)}, f32[4096,256]{0,1:T(8,128)}, s32[]{:T(128)}, /*index=5*/s32...) while((s32[]{:T(128)}, f32[128,1,8,128]{3,0,2,1:T(8,128)}, ...), condition=%wide.region_15.16_spmd.clone.clone, body=%wide.region_10.15_spmd.clone.clone.sunk | while | flops 1350440704 | bytes 36462060 | solution.py:254
  185.5 4.5 conditional.13
  189.9 4.5 conditional.12
  203.5 4.5 conditional.13
  208.0 4.5 conditional.12
  221.6 4.5 conditional.13
  226.0 4.5 conditional.12
  236.8 4.0 convert_element_type.84
  240.8 119.8 %reduce-scatter.9.cloned.1.call-done = bf16[1024,256]{0,1:T(8,128)(2,1)} async-done(((bf16[4096,256]{0,1:T(8,128)(2,1)}), bf16[1024,256]{0,1:T(8,128)(2,1)}) %reduce-scatter.9.cloned.1.call-update) | async-done | bytes 524304 | tf_op jit(solution)/shard_map/reduce_scatter | solution.py:30
  363.8 37.8 %reduce-scatter.13.cloned.1.call-done = bf16[128,256]{1,0:T(8,128)(2,1)} async-done(((bf16[1024,256]{1,0:T(8,128)(2,1)}), bf16[128,256]{1,0:T(8,128)(2,1)}) %reduce-scatter.13.cloned.1.call-update) | async-done | bytes 65552
  405.3 29.2 %reduce-scatter.11.cloned.1.call-done = bf16[1024,256]{0,1:T(8,128)(2,1)} async-done(((bf16[4096,256]{0,1:T(8,128)(2,1)}), bf16[1024,256]{0,1:T(8,128)(2,1)}) %reduce-scatter.11.cloned.1.call-update) | async-done | bytes 524304 | tf_op jit(solution)/shard_map/reduce_scatter | solution.py:49
  438.7 76.9 %all-gather.5.cloned.1.call-done = bf16[4096,256]{1,0:T(8,128)(2,1)} async-done(((bf16[128,256]{1,0:T(8,128)(2,1)}), bf16[4096,256]{1,0:T(8,128)(2,1)}) %all-gather.5.cloned.1.call-update) | async-done | bytes 2097168 | tf_op jit(solution)/shard_map/all_gather | solution.py:281
  518.2 5.4 all_to_all.26
  523.6 30.1 %reduce-scatter.15.cloned.1.call-done = bf16[128,256]{1,0:T(8,128)(2,1)} async-done(((bf16[1024,256]{1,0:T(8,128)(2,1)}), bf16[128,256]{1,0:T(8,128)(2,1)}) %reduce-scatter.15.cloned.1.call-update) | async-done | bytes 65552 | tf_op jit(solution)/shard_map/reduce_scatter | solution.py:49
  555.3 4.2 all-to-all-start.4
  (208 shorter events, 124.4 us)
Async XLA Ops:
  10.2 6.6 %all-to-all-start.1 = ((bf16[2,256,2048]{1,2,0:T(8,128)(2,1)}), bf16[2,256,2048]{1,2,0:T(8,128)(2,1)S(1)}, u32[]{:S(2)}, u32[]{:S(2)}) async-start(bf16[2,256,2048]{1,2,0:T(8,128)(2,1)} %broadcast_in_dim.134), calls=%async_computation.1 | async-start | bytes 4194304 | tf_op jit(solution)/shard_map/all_to_all | solution.py:21
  14.0 64.2 %copy-start.15 = (bf16[128,256]{1,0:T(8,128)(2,1)}, bf16[128,256]{1,0:T(8,128)(2,1)S(1)}, u32[]{:S(2)}) copy-start(bf16[128,256]{1,0:T(8,128)(2,1)S(1)} %constant_dynamic-update-slice_fusion.1) | copy-start | bytes 196612
  16.8 61.4 %copy-start.4 = (bf16[2,256,2048]{1,2,0:T(8,128)(2,1)}, bf16[2,256,2048]{1,2,0:T(8,128)(2,1)S(1)}, u32[]{:S(2)}) copy-start(bf16[2,256,2048]{1,2,0:T(8,128)(2,1)S(1)} %all-to-all-done.1) | copy-start | bytes 6291460
  78.2 12.9 %copy-start.16 = (bf16[256,256]{0,1:T(8,128)(2,1)}, bf16[256,256]{0,1:T(8,128)(2,1)S(1)}, u32[]{:S(2)}) copy-start(bf16[256,256]{0,1:T(8,128)(2,1)S(1)} %fusion.92) | copy-start | bytes 393220
  78.2 10.8 %copy-start.14 = (bf16[1,2,128,1024]{3,2,1,0:T(8,128)(2,1)S(1)}, bf16[1,2,128,1024]{3,2,1,0:T(8,128)(2,1)}, u32[]{:S(2)}) copy-start(bf16[1,2,128,1024]{3,2,1,0:T(8,128)(2,1)} %param.17) | copy-start | bytes 1572868
  78.2 9.4 %copy-start.13 = (bf16[128,256]{0,1:T(8,128)(2,1)}, bf16[128,256]{0,1:T(8,128)(2,1)S(1)}, u32[]{:S(2)}) copy-start(bf16[128,256]{0,1:T(8,128)(2,1)S(1)} %slice.67) | copy-start | bytes 196612
  79.9 57.5 %all-to-all-start.2 = ((bf16[32,128,256]{2,1,0:T(8,128)(2,1)}), bf16[32,128,256]{2,1,0:T(8,128)(2,1)S(1)}, u32[]{:S(2)}, u32[]{:S(2)}) async-start(bf16[32,128,256]{2,1,0:T(8,128)(2,1)} %broadcast_in_dim.135), calls=%async_computation.2 | async-start | bytes 4194304 | tf_op jit(solution)/shard_map/all_to_all | solution.py:21
  87.5 91.0 %all-gather.3.cloned.1.call-start = ((), (), s32[]{:S(2)}) async-start(), calls=%async_computation.9 | async-start | bytes 2162688 | tf_op jit(solution)/shard_map/all_gather | solution.py:198
  88.3 272.4 %reduce-scatter.9.cloned.1.call-start = ((), (), s32[]{:S(2)}) async-start(), calls=%async_computation.10 | async-start | bytes 2621440 | tf_op jit(solution)/shard_map/reduce_scatter | solution.py:30
  89.2 49.8 %copy-start.8 = (bf16[1,1,128,1024]{2,3,1,0:T(8,128)(2,1)}, bf16[1,1,128,1024]{2,3,1,0:T(8,128)(2,1)S(1)}, u32[]{:S(2)}) copy-start(bf16[1,1,128,1024]{2,3,1,0:T(8,128)(2,1)S(1)} %copy.165) | copy-start | bytes 786436
  91.1 6.7 %copy-start.17 = (bf16[256,256]{0,1:T(8,128)(2,1)S(1)}, bf16[256,256]{0,1:T(8,128)(2,1)}, u32[]{:S(2)}) copy-start(bf16[256,256]{0,1:T(8,128)(2,1)} %copy-done.16) | copy-start | bytes 393220
  91.3 86.1 %copy-start.6 = (bf16[1,1,128,1024]{2,3,1,0:T(8,128)(2,1)}, bf16[1,1,128,1024]{2,3,1,0:T(8,128)(2,1)S(1)}, u32[]{:S(2)}) copy-start(bf16[1,1,128,1024]{2,3,1,0:T(8,128)(2,1)S(1)} %copy.166) | copy-start | bytes 786436
  236.8 126.3 %copy-start.3 = (f32[1,8,128,128]{2,3,1,0:T(8,128)S(1)}, f32[1,8,128,128]{2,3,1,0:T(8,128)}, u32[]{:S(2)}) copy-start(f32[1,8,128,128]{2,3,1,0:T(8,128)} %copy-done.2) | copy-start | bytes 1572868
  236.8 126.3 %copy-start.7 = (bf16[1,1,128,1024]{2,3,1,0:T(8,128)(2,1)S(1)}, bf16[1,1,128,1024]{2,3,1,0:T(8,128)(2,1)}, u32[]{:S(2)}) copy-start(bf16[1,1,128,1024]{2,3,1,0:T(8,128)(2,1)} %copy-done.6) | copy-start | bytes 786436
  236.8 126.5 %copy-start.9 = (bf16[1,1,128,1024]{2,3,1,0:T(8,128)(2,1)S(1)}, bf16[1,1,128,1024]{2,3,1,0:T(8,128)(2,1)}, u32[]{:S(2)}) copy-start(bf16[1,1,128,1024]{2,3,1,0:T(8,128)(2,1)} %copy-done.8) | copy-start | bytes 786436
  240.8 161.8 %copy-start.5 = (bf16[2,256,2048]{1,2,0:T(8,128)(2,1)S(1)}, bf16[2,256,2048]{1,2,0:T(8,128)(2,1)}, u32[]{:S(2)}) copy-start(bf16[2,256,2048]{1,2,0:T(8,128)(2,1)} %copy-done.4) | copy-start | bytes 6291460
  240.8 160.8 %reduce-scatter.13.cloned.1.call-start = ((), (), s32[]{:S(2)}) async-start(), calls=%async_computation.13 | async-start | bytes 589824
  362.7 71.7 %reduce-scatter.11.cloned.1.call-start = ((), (), s32[]{:S(2)}) async-start(), calls=%async_computation.12 | async-start | bytes 2621440 | tf_op jit(solution)/shard_map/reduce_scatter | solution.py:49
  363.8 72.7 %copy-start.1 = (f32[128,1,8,128]{3,0,2,1:T(8,128)S(1)}, f32[128,1,8,128]{3,0,2,1:T(8,128)}, u32[]{:S(2)}) copy-start(f32[128,1,8,128]{3,0,2,1:T(8,128)} %get-tuple-element.441) | copy-start | bytes 1572868
  402.6 34.2 %copy-start = (f32[128,1,8,128]{3,0,2,1:T(8,128)S(1)}, f32[128,1,8,128]{3,0,2,1:T(8,128)}, u32[]{:S(2)}) copy-start(f32[128,1,8,128]{3,0,2,1:T(8,128)} %get-tuple-element.440) | copy-start | bytes 1572868
  404.7 110.9 %all-gather.5.cloned.1.call-start = ((), (), s32[]{:S(2)}) async-start(), calls=%async_computation.11 | async-start | bytes 2162688 | tf_op jit(solution)/shard_map/all_gather | solution.py:281
  405.3 148.5 %reduce-scatter.15.cloned.1.call-start = ((), (), s32[]{:S(2)}) async-start(), calls=%async_computation.14 | async-start | bytes 589824 | tf_op jit(solution)/shard_map/reduce_scatter | solution.py:49
  518.0 41.7 %copy-start.12 = (bf16[128,1,8,128]{0,3,2,1:T(8,128)(2,1)S(1)}, bf16[128,1,8,128]{0,3,2,1:T(8,128)(2,1)}, u32[]{:S(2)}) copy-start(bf16[128,1,8,128]{0,3,2,1:T(8,128)(2,1)} %fusion.88) | copy-start | bytes 786436
  555.3 10.9 %all-to-all-start.4 = ((bf16[4,128,256]{2,1,0:T(8,128)(2,1)}), bf16[4,128,256]{2,1,0:T(8,128)(2,1)S(1)}, u32[]{:S(2)}, u32[]{:S(2)}) async-start(bf16[4,128,256]{2,1,0:T(8,128)(2,1)} %broadcast_in_dim.144), calls=%async_computation.6 | async-start | bytes 524288 | tf_op jit(solution)/shard_map/all_to_all | solution.py:21
  (7 other events, 19.4 us)
Sparse Core Ops, SparseCore 0:
  91.4 84.0 all-gather.2
  240.9 119.6 reduce-scatter.8
  363.3 38.2 reduce-scatter.12
  404.8 29.6 reduce-scatter.10
  437.8 77.7 all-gather.4
  518.1 35.6 reduce-scatter.14
